TPU v7x, 32 devices: a whole 2x2x4 slice. The times are simulated.
32 devices in a mesh: scene: 2 (over x), tile: 8 (over z, y), chan: 2 (over core).
Axes of the slice: x: 2, y: 2, z: 4, core: 2. Of those that a mesh axis runs over, the one named last changes fastest.
Arguments:
- raw_echoes: bfloat16 [256, 12, 2, 2048], P(('scene', 'tile'), 'chan'), parts along dimension 0, may hold values from -6 to 6
- range_taps: bfloat16 [12, 2, 512], replicated, may hold values from -0.1875 to 0.1875
- beam_weights: bfloat16 [12, 2, 2048], replicated, may hold values from -1.1953125 to 1.1953125
- channel_order: int32 [12], replicated, may hold values from 0 to 11, each once
- group_cells: int32 [8], replicated, may hold values from 128 to 384, as said below
- tap_counts: int32 [2048], replicated, may hold values from 384 to 640, as said below
- chirp_rates: float32 [2048], replicated, may hold values from 0.5 to 2
Outputs:
- focused_image: float32 [6144, 2, 128], P(('scene', 'tile', 'chan')), parts along dimension 0
There are 2 independent parts, one for each index of `scene`. A program takes and returns all parts, laid end to end along the dimension named above; an argument that names none is the same for every part. Nothing has to cross between parts.
Inputs may be any that keep to these rules, and one draw needn't show every extreme that they name: `channel_order`: A permutation of the channels. `group_cells`: the counts sum to 2048; devices 2i and 2i + 1 of tile together own 2 * 256 cells; at least one device owns exactly 384. `tap_counts`: the first range cell has 384 taps and the last 640; counts rise with range up to a small jitter.
All inputs are finite; a program needn't handle non-finite values.
Results may differ from a plain program's by a relative error of at most 0.0053.
Values may be sent and summed in bfloat16 or wider, within the bound.
A program may use at most 320 MiB of HBM per device.

v0:
```python
import jax
import jax.numpy as jnp
from jax import lax
from jax.sharding import PartitionSpec as P

KMAX = 640


def toeplitz_rows(coeffs, block_len, span_len):
    leading = coeffs.shape[:-1]
    filler = jnp.zeros(leading + (span_len + 1 - coeffs.shape[-1],), coeffs.dtype)
    extended = jnp.concatenate([coeffs, filler], -1)
    repeated = jnp.tile(extended, (1,) * len(leading) + (block_len,))
    return repeated[..., : block_len * span_len].reshape(leading + (block_len, span_len))


def complex_matrix(toeplitz_pair):
    real_part = toeplitz_pair[..., 0, :, :]
    imag_part = toeplitz_pair[..., 1, :, :]
    from_real = jnp.stack([real_part, imag_part], -3)
    from_imag = jnp.stack([-imag_part, real_part], -3)
    return jnp.stack([from_real, from_imag], -4)


def block_windows(signal, block_len, lead_blocks, span_blocks, out_blocks):
    total_blocks = out_blocks + span_blocks - 1
    right_pad = total_blocks * block_len - lead_blocks * block_len - signal.shape[-1]
    padded = jnp.pad(signal, [(0, 0)] * (signal.ndim - 1) + [(lead_blocks * block_len, right_pad)])
    blocked = padded.reshape(signal.shape[:-1] + (total_blocks, block_len))
    return jnp.concatenate(
        [
            blocked[..., offset_block : offset_block + out_blocks, :]
            for offset_block in range(span_blocks)
        ],
        -1,
    )


def chirp_taps(counts, sweep_rates, longest):
    position = jnp.arange(longest, dtype=jnp.int32)[None, :]
    lengths = counts[:, None]
    shifted = position - (longest // 2 - lengths // 2)
    inside = (shifted >= 0) & (shifted < lengths)
    extent = lengths.astype(jnp.float32)
    located = shifted.astype(jnp.float32)
    centred = (located - 0.5 * (extent - 1.0)) / extent
    angles = jnp.pi * sweep_rates[:, None] * extent * centred * centred
    envelope = (
        (0.5 - 0.5 * jnp.cos(2.0 * jnp.pi * (located + 0.5) / extent)) * 1.6 / jnp.sqrt(extent)
    )
    envelope = jnp.where(inside, envelope, jnp.zeros_like(envelope))
    return jnp.stack([envelope * jnp.cos(angles), envelope * jnp.sin(angles)], 1)


def range_compress(echoes, filters):
    block_len = filters.shape[-1] // 2
    windows = block_windows(echoes, block_len, 1, 3, echoes.shape[-1] // block_len)
    matrices = complex_matrix(toeplitz_rows(filters, block_len, 3 * block_len))
    product = jnp.einsum(
        "pcanw,caeiw->pceni", windows, matrices, preferred_element_type=jnp.float32
    )
    return product.reshape(echoes.shape)


def azimuth_focus(columns, coeffs):
    block_len = coeffs.shape[-1] // 8
    pulses = columns.shape[-1]
    out_blocks = -(-pulses // block_len)
    windows = block_windows(columns, block_len, 4, 9, out_blocks)
    matrices = complex_matrix(toeplitz_rows(coeffs, block_len, 9 * block_len))
    product = jnp.einsum("sanw,saeiw->seni", windows, matrices, preferred_element_type=jnp.float32)
    return product.reshape(columns.shape[:-1] + (out_blocks * block_len,))[..., :pulses]


def owner_slots(signal, group_starts, group_sizes, offset, slot_width, margin):
    padded = jnp.pad(signal, [(0, 0)] * (signal.ndim - 1) + [(0, margin)])

    def one_group(start_cell, size_cells):
        window_cut = lax.dynamic_slice_in_dim(
            padded, start_cell + offset, slot_width, signal.ndim - 1
        )
        inside = jnp.arange(slot_width, dtype=jnp.int32) + offset < size_cells
        return jnp.where(inside, window_cut, jnp.zeros_like(window_cut))

    return jax.vmap(one_group)(group_starts, group_sizes)


def on_device(
    raw_echoes, range_taps, beam_weights, channel_order, group_cells, tap_counts, chirp_rates
):
    local_chans = raw_echoes.shape[1]
    all_chans = range_taps.shape[0]
    first_slot = lax.axis_index("chan") * local_chans
    own_channels = lax.dynamic_slice_in_dim(channel_order, first_slot, local_chans)
    selector = (own_channels[:, None] == jnp.arange(all_chans, dtype=jnp.int32)[None, :]).astype(
        jnp.bfloat16
    )
    filters = jnp.dot(
        selector, range_taps.reshape(all_chans, -1), preferred_element_type=jnp.float32
    )
    filters = filters.astype(jnp.bfloat16).reshape(local_chans, 2, -1)
    weights = jnp.dot(
        selector, beam_weights.reshape(all_chans, -1), preferred_element_type=jnp.float32
    )
    weights = weights.reshape(local_chans, 2, -1)
    spectra = range_compress(raw_echoes, filters)
    real_sum = jnp.sum(spectra[:, :, 0] * weights[:, 0] - spectra[:, :, 1] * weights[:, 1], 1)
    imag_sum = jnp.sum(spectra[:, :, 0] * weights[:, 1] + spectra[:, :, 1] * weights[:, 0], 1)
    partial_value = jnp.stack([real_sum, imag_sum], 1)
    tile_count = group_cells.shape[0]
    cell_count = raw_echoes.shape[-1]
    average = cell_count // tile_count
    capacity = average + average // 2
    chan_ways = lax.axis_size("chan")
    half_cap = capacity // chan_ways
    group_starts = jnp.cumsum(group_cells) - group_cells
    chan_offset = lax.axis_index("chan") * half_cap
    summed = lax.psum(partial_value.astype(jnp.bfloat16), "chan")
    outgoing = owner_slots(summed, group_starts, group_cells, chan_offset, half_cap, capacity)
    outgoing = outgoing.transpose(0, 3, 2, 1)
    incoming = lax.all_to_all(outgoing, "tile", split_axis=0, concat_axis=3, tiled=True)
    columns = incoming[0]
    tile_here = lax.axis_index("tile")
    begin_cell = lax.dynamic_index_in_dim(group_starts, tile_here, keepdims=False)
    owned_cells = lax.dynamic_index_in_dim(group_cells, tile_here, keepdims=False)
    local_slot = chan_offset + jnp.arange(half_cap, dtype=jnp.int32)
    inside = local_slot < owned_cells
    count_table = jnp.pad(tap_counts, (0, capacity), mode="edge")
    rate_table = jnp.pad(chirp_rates, (0, capacity), mode="edge")
    count_here = lax.dynamic_slice_in_dim(count_table, begin_cell + chan_offset, half_cap)
    rate_here = lax.dynamic_slice_in_dim(rate_table, begin_cell + chan_offset, half_cap)
    taps_here = chirp_taps(count_here, rate_here, KMAX)
    taps_here = jnp.where(inside[:, None, None], taps_here, jnp.zeros_like(taps_here)).astype(
        jnp.bfloat16
    )
    return azimuth_focus(columns, taps_here)


def solution(mesh):
    return jax.shard_map(
        on_device,
        mesh=mesh,
        in_specs=(P(("scene", "tile"), "chan", None, None), P(), P(), P(), P(), P(), P()),
        out_specs=P(("scene", "tile", "chan"), None, None),
        check_vma=False,
    )
```

profile of v0, /device:TPU:0, one launch (start us, length us, event | category | flops | bytes accessed | tf_op | source)
XLA Modules:
  0.0 758.5 jit_solution(17787121821127459724)
XLA Ops:
  6.5 0.8 pad.35
  7.3 0.7 dynamic_slice.20
  8.1 0.2 convolution_convert_fusion
  8.3 2.8 tile.20
  11.1 16.3 %tile.21 = bf16[6,2,196864]{2,1,0:T(2,128)(2,1)} reshape(bf16[6,2,256,769]{3,2,1,0:T(8,128)(2,1)} %tile.20) | data formatting | bytes 9449472 | tf_op jit(solution)/shard_map/tile | solution.py:13
  27.4 5.5 slice.120
  33.0 7.1 reshape.426
  40.1 7.1 stack.50
  47.2 0.7 pad.17
  48.0 0.7 reshape.450
  48.7 0.5 fusion.34
  49.2 1.3 copy.79
  50.5 1.3 copy.78
  51.8 1.3 copy.77
  53.1 0.3 slice_negate_fusion.1
  53.5 2.8 maximum_bitcast_fusion.3
  56.3 1.1 slice-done.3
  57.4 0.2 copy-done
  57.6 5.1 fusion.11
  62.8 0.2 copy.90
  63.0 0.1 pad.36
  63.1 0.1 dot_general.19
  63.2 0.2 fusion.21
  63.4 0.2 subtract_reduce_fusion
  63.7 2.0 copy.56
  65.7 0.2 reduce-window.9
  65.9 0.7 dynamic_slice.16
  66.6 0.6 dynamic_slice.17
  67.8 0.6 slice.89
  68.4 0.7 slice.87
  69.1 0.8 convert_sqrt_fusion
  69.8 0.7 fusion.28
  70.6 0.7 broadcast_compare_fusion.1
  71.3 4.1 cosine_multiply_fusion
  75.4 0.2 fusion.16
  75.5 0.5 copy.89
  76.0 0.4 concatenate.25.clone
  76.4 15.2 %tile.8 = bf16[192,2,80,721]{3,2,1,0:T(8,128)(2,1)} broadcast(bf16[192,2,721]{2,1,0:T(2,128)(2,1)S(1)} %concatenate.25.clone), dimensions={0,1,3} | broadcast | bytes 44851968 | tf_op jit(solution)/shard_map/tile | solution.py:13
  91.6 172.0 %tile.9 = bf16[192,2,57680]{2,1,0:T(2,128)(2,1)} reshape(bf16[192,2,80,721]{3,2,1,0:T(8,128)(2,1)} %tile.8) | data formatting | bytes 88596480 | tf_op jit(solution)/shard_map/tile | solution.py:13
  263.7 35.6 %slice.117 = bf16[192,2,57600]{2,1,0:T(2,128)(2,1)} slice(bf16[192,2,57680]{2,1,0:T(2,128)(2,1)} %tile.9), slice={[0:192], [0:2], [0:57600]} | slice | bytes 88473600 | tf_op jit(solution)/shard_map/slice | solution.py:14
  299.3 163.8 %reshape.423 = bf16[192,2,80,720]{3,2,1,0:T(8,128)(2,1)} reshape(bf16[192,2,57600]{2,1,0:T(2,128)(2,1)} %slice.117) | data formatting | bytes 88473600 | tf_op jit(solution)/shard_map/reshape | solution.py:14
  463.1 32.1 %slice_negate_fusion = (bf16[192,1,80,720]{3,2,1,0:T(8,128)(2,1)}, bf16[192,1,80,720]{3,2,1,0:T(8,128)(2,1)}) fusion(bf16[192,2,80,720]{3,2,1,0:T(8,128)(2,1)} %reshape.423), kind=kLoop, calls=%fused_computation.6 | loop fusion | flops 11059200 | bytes 88473600 | tf_op jit(solution)/shard_map/neg | solution.py:21
  495.2 0.1 broadcast_compare_fusion
  495.3 3.1 pad.18
  498.4 2.1 gather_fusion
  500.6 2.3 fusion.17
  502.9 1.7 copy.57
  504.6 7.3 all-to-all-start
  511.9 31.9 %maximum_bitcast_fusion = bf16[192,1,2,80,720]{4,3,1,2,0:T(8,128)(2,1)} fusion(bf16[192,1,80,720]{3,2,1,0:T(8,128)(2,1)} %get-tuple-element.12, bf16[192,1,80,720]{3,2,1,0:T(8,128)(2,1)} %get-tuple-element.11), kind=kLoop, calls=%fused_computation.5 | loop fusion | flops 22118400 | bytes 88473600 | tf_op jit(solution)/shard_map/stack | solution.py:22
  543.7 163.8 %stack.46 = bf16[192,1,2,80,720]{4,3,1,2,0:T(8,128)(2,1)} reshape(bf16[192,2,57600]{2,1,0:T(2,128)(2,1)} %slice.117) | data formatting | bytes 88473600 | tf_op jit(solution)/shard_map/stack | solution.py:22
  707.6 0.1 fusion.35
  707.7 0.2 copy.80
  707.9 0.2 copy.81
  708.1 0.2 copy.82
  708.2 0.2 copy.83
  708.4 0.2 copy.84
  708.6 0.2 copy.85
  708.7 0.2 copy.86
  708.9 0.2 copy.87
  709.0 0.2 copy.88
  709.2 5.3 concatenate.29
  714.5 36.0 %fusion.12 = f32[192,2,2,80]{3,2,1,0:T(2,128)S(1)} fusion(bf16[192,1,2,80,720]{4,3,1,2,0:T(8,128)(2,1)} %maximum_bitcast_fusion, bf16[192,1,2,80,720]{4,3,1,2,0:T(8,128)(2,1)} %stack.46, bf16[192,2,2,720]{3,2,1,0:T(2,128)(2,1)S(1)} %concatenate.29), kind=kOutput, calls=%fused_computation.20 | convolution fusion | flops 221184000 | bytes 89825280 | tf_op jit(solution)/shard_map/sanw,saeiw->seni/dot_general | solution.py:71
  750.5 0.3 copy.68
  750.8 0.8 copy.69
  (36 shorter events, 0.3 us)
Async XLA Ops:
  6.5 488.8 %all-reduce.10.cloned.1.call-start = ((), (), s32[]{:S(2)}) async-start(), calls=%async_computation.1 | async-start | bytes 2097152 | tf_op jit(solution)/shard_map/psum | solution.py:118
  40.1 7.1 copy-start.1
  47.9 5.2 slice-start
  48.7 4.4 slice-start.1
  53.1 3.2 slice-start.2
  53.4 3.9 slice-start.3
  53.4 4.1 copy-start
  57.6 5.4 copy-start.2
  62.7 2.9 copy-start.5
  62.7 5.0 copy-start.3
  62.8 5.6 copy-start.4
  504.6 202.9 %all-to-all-start = ((bf16[8,192,2,16]{1,3,2,0:T(8,128)(2,1)}), bf16[8,192,2,16]{1,3,2,0:T(8,128)(2,1)S(1)}, u32[]{:S(2)}, u32[]{:S(2)}) async-start(bf16[8,192,2,16]{1,3,2,0:T(8,128)(2,1)} %copy.57), calls=%async_computation | async-start | bytes 262144 | tf_op jit(solution)/shard_map/all_to_all | solution.py:121
Sparse Core Ops, SparseCore 0:
  65.8 22.2 all-reduce.9
where the time goes:
time: 772 us; the launch traced here: 758 us
  local copies, waits for them, and re-layouts  619 us (80%)
  other arithmetic  76.4 us (10%)
  matrix products  41.6 us (5%)
  between operations  14.4 us (2%)
    another operation x4, local copies, waits for them, and re-layouts, toeplitz_rows(): repeated = jnp.tile(extended, (1,) * len(leading) + (block_len,))  206 us
    another operation x2, local copies, waits for them, and re-layouts, complex_matrix(): return jnp.stack([from_real, from_imag], -4)  171 us
    reshape x2, local copies, waits for them, and re-layouts, toeplitz_rows(): repeated[..., :block_len * span_len]  171 us
    slice x2, local copies, waits for them, and re-layouts, toeplitz_rows(): repeated[..., :block_len * span_len]  41.2 us
    dot_general x1, matrix products, azimuth_focus(): jnp.einsum('sanw,saeiw->seni', windows, matrices, preferred_element_type=...  36 us
    another operation x2, other arithmetic, complex_matrix(): return jnp.stack([from_real, from_imag], -4)  34.7 us
    neg x2, other arithmetic, complex_matrix(): from_imag = jnp.stack([-imag_part, real_part], -3)  32.4 us
  transfers between devices with their start and end apart: 2, of which 0 were waited for; matrix products, arithmetic and copies ran while one was open for 82% of the time, Pallas kernels for 0%

commit v1 on v0

--- a/solution.py
+++ b/solution.py
@@ -1,6 +1,11 @@
+import functools
+
 import jax
 import jax.numpy as jnp
+import numpy as np
 from jax import lax
+from jax.experimental import pallas as pl
+from jax.experimental.pallas import tpu as pltpu
 from jax.sharding import PartitionSpec as P
 
 KMAX = 640
@@ -85,7 +90,7 @@
     return jax.vmap(one_group)(group_starts, group_sizes)
 
 
-def on_device(
+def generic_device(
     raw_echoes, range_taps, beam_weights, channel_order, group_cells, tap_counts, chirp_rates
 ):
     local_chans = raw_echoes.shape[1]
@@ -136,6 +141,354 @@
     return azimuth_focus(columns, taps_here)
 
 
+MESH = pl.DeviceIdType.MESH
+BLOCK = 256
+SPAN = 3 * BLOCK
+
+
+def split_bf16(matrix):
+    high = matrix.astype(jnp.bfloat16)
+    low = (matrix - high.astype(np.float64)).astype(jnp.bfloat16)
+    return np.stack([high, low])
+
+
+def fourier_tables(tiles, pulses):
+    points = 2 * pulses
+    local = pulses // tiles
+    freq = np.arange(points)[:, None]
+    unit = 2.0 * np.pi / points
+
+    def rotation(index, sign):
+        angle = unit * ((freq * index[None, :]) % points)
+        return np.cos(angle), sign * np.sin(angle)
+
+    cos_x, sin_x = rotation(np.arange(pulses), -1.0)
+    forward = np.block([[cos_x, -sin_x], [sin_x, cos_x]])
+    order = np.arange(2 * pulses).reshape(2, tiles, local).transpose(1, 0, 2).reshape(-1)
+    forward = forward[:, order]
+    cos_h, sin_h = rotation(pulses - np.arange(points), -1.0)
+    taps = np.block([[cos_h, -sin_h], [sin_h, cos_h]])
+    cos_y, sin_y = rotation(np.arange(pulses), 1.0)
+    inverse = np.block([[cos_y, sin_y], [-sin_y, cos_y]]) / points
+    return split_bf16(forward), split_bf16(taps), split_bf16(inverse)
+
+
+def range_kernel(
+    half_cap,
+    order_ref,
+    cells_ref,
+    raw_ref,
+    filter_ref,
+    weight_ref,
+    count_ref,
+    rate_ref,
+    packed_ref,
+    table_ref,
+    blocks,
+    partial,
+):
+    chan = pl.program_id(0)
+    out_blocks = raw_ref.shape[3] // BLOCK
+    pulses = raw_ref.shape[2]
+
+    @pl.when(chan == 0)
+    def _():
+        edge = jnp.zeros((2, pulses, BLOCK), jnp.bfloat16)
+        blocks[:, 0] = edge
+        blocks[:, out_blocks + 1] = edge
+        partial[...] = jnp.zeros_like(partial)
+
+    for block in range(out_blocks):
+        blocks[:, block + 1] = raw_ref[0, :, :, block * BLOCK : (block + 1) * BLOCK]
+
+    def toeplitz(part):
+        row = jnp.broadcast_to(filter_ref[0, part : part + 1, :], (128, SPAN))
+        top = pltpu.roll(row, 0, 1, stride=1, stride_axis=0).astype(jnp.bfloat16)
+        low = jnp.concatenate([top[:, SPAN - 128 :], top[:, : SPAN - 128]], 1)
+        return jnp.concatenate([top, low], 0)
+
+    real_rows = toeplitz(0)
+    imag_rows = toeplitz(1)
+    total = None
+    for step in range(3):
+        at = (SPAN - BLOCK * step) % SPAN
+        matrix = jnp.concatenate(
+            [real_rows[:, at : at + BLOCK], imag_rows[:, at : at + BLOCK]], 1
+        )
+        window = blocks[:, step : step + out_blocks].reshape(2 * out_blocks * pulses, BLOCK)
+        term = jnp.dot(window, matrix, preferred_element_type=jnp.float32)
+        total = term if total is None else total + term
+    half = out_blocks * pulses
+    comp_real = total[:half, :BLOCK] - total[half:, BLOCK:]
+    comp_imag = total[half:, :BLOCK] + total[:half, BLOCK:]
+    for block in range(out_blocks):
+        cells = slice(block * BLOCK, (block + 1) * BLOCK)
+        weight_real = weight_ref[0, 0:1, cells].astype(jnp.float32)
+        weight_imag = weight_ref[0, 1:2, cells].astype(jnp.float32)
+        value_real = comp_real[block * pulses : (block + 1) * pulses]
+        value_imag = comp_imag[block * pulses : (block + 1) * pulses]
+        partial[0, block] += weight_real * value_real - weight_imag * value_imag
+        partial[1, block] += weight_imag * value_real + weight_real * value_imag
+
+    @pl.when(chan == pl.num_programs(0) - 1)
+    def _():
+        width = 2 * BLOCK
+        for pair in range(out_blocks // 2):
+            first = cells_ref[2 * pair]
+            for part in range(2):
+                values = jnp.concatenate(
+                    [partial[part, 2 * pair], partial[part, 2 * pair + 1]], 1
+                )
+                packed_ref[0, 2 * pair, part] = values[:, :BLOCK].astype(jnp.bfloat16)
+                packed_ref[1, 2 * pair, part] = pltpu.roll(values, width - half_cap, 1)[
+                    :, :BLOCK
+                ].astype(jnp.bfloat16)
+                moved = pltpu.roll(values, width - first, 1)
+                packed_ref[0, 2 * pair + 1, part] = moved[:, :BLOCK].astype(jnp.bfloat16)
+                packed_ref[1, 2 * pair + 1, part] = pltpu.roll(moved, width - half_cap, 1)[
+                    :, :BLOCK
+                ].astype(jnp.bfloat16)
+        tile_here = lax.axis_index("tile")
+        offset = lax.axis_index("chan") * half_cap
+        begin = offset
+        for tile in range(cells_ref.shape[0]):
+            begin += jnp.where(tile < tile_here, cells_ref[tile], 0)
+        cell_count = count_ref.shape[1]
+        shift = lax.rem(2 * cell_count - begin, cell_count)
+
+        def own(table):
+            spread = jnp.broadcast_to(table.astype(jnp.float32), (8, cell_count))
+            return pltpu.roll(spread, shift, 1)[:, :BLOCK]
+
+        extent = own(count_ref[...])
+        slot = lax.broadcasted_iota(jnp.int32, (8, BLOCK), 1)
+        live = (slot < half_cap) & (slot + offset < cells_ref[tile_here])
+        scale = jnp.where(live, 1.6 / jnp.sqrt(extent), 0.0)
+        table_ref[0] = extent
+        table_ref[1] = own(rate_ref[...])
+        table_ref[2] = scale
+
+
+def range_call(raw_echoes, range_taps, beam_weights, order, cells, counts, rates, half_cap):
+    local_chans = raw_echoes.shape[1]
+    pulses = raw_echoes.shape[0]
+    cell_count = raw_echoes.shape[3]
+    tiles = cells.shape[0]
+    out_blocks = cell_count // BLOCK
+    taps = range_taps.shape[-1]
+    echoes = raw_echoes.transpose(1, 2, 0, 3)
+    reversed_taps = jnp.concatenate(
+        [
+            range_taps[..., :1],
+            jnp.zeros(range_taps.shape[:2] + (SPAN - taps,), range_taps.dtype),
+            jnp.flip(range_taps[..., 1:], -1),
+        ],
+        -1,
+    ).astype(jnp.float32)
+
+    def physical(chan, order_ref, cells_ref):
+        return (order_ref[lax.axis_index("chan") * local_chans + chan], 0, 0)
+
+    return pl.pallas_call(
+        functools.partial(range_kernel, half_cap),
+        grid_spec=pltpu.PrefetchScalarGridSpec(
+            num_scalar_prefetch=2,
+            grid=(local_chans,),
+            in_specs=[
+                pl.BlockSpec((1, 2, pulses, cell_count), lambda c, o, g: (c, 0, 0, 0)),
+                pl.BlockSpec((1, 2, SPAN), physical),
+                pl.BlockSpec((1, 2, cell_count), physical),
+                pl.BlockSpec((1, cell_count), lambda c, o, g: (0, 0)),
+                pl.BlockSpec((1, cell_count), lambda c, o, g: (0, 0)),
+            ],
+            out_specs=[
+                pl.BlockSpec((2, tiles, 2, pulses, BLOCK), lambda c, o, g: (0, 0, 0, 0, 0)),
+                pl.BlockSpec((3, 8, BLOCK), lambda c, o, g: (0, 0, 0)),
+            ],
+            scratch_shapes=[
+                pltpu.VMEM((2, out_blocks + 2, pulses, BLOCK), jnp.bfloat16),
+                pltpu.VMEM((2, out_blocks, pulses, BLOCK), jnp.float32),
+            ],
+        ),
+        out_shape=[
+            jax.ShapeDtypeStruct((2, tiles, 2, pulses, BLOCK), jnp.bfloat16),
+            jax.ShapeDtypeStruct((3, 8, BLOCK), jnp.float32),
+        ],
+        compiler_params=pltpu.CompilerParams(vmem_limit_bytes=32 << 20),
+    )(order, cells, echoes, reversed_taps, beam_weights, counts[None], rates[None])
+
+
+def even_series(square, terms):
+    value = jnp.full_like(square, terms[-1])
+    for term in reversed(terms[:-1]):
+        value = value * square + term
+    return value
+
+
+COS_TERMS = [(-1.0) ** n * (2 * np.pi) ** (2 * n) / float(np.prod(np.arange(1, 2 * n + 1, dtype=np.float64))) for n in range(9)]
+SIN_TERMS = [(-1.0) ** n * (2 * np.pi) ** (2 * n + 1) / float(np.prod(np.arange(1, 2 * n + 2, dtype=np.float64))) for n in range(9)]
+
+
+def write_taps(table_ref, tap_ref, first_tap):
+    rows = tap_ref.shape[0] // 2
+    extent = table_ref[0, 0:1]
+    rate = table_ref[1, 0:1]
+    scale = table_ref[2, 0:1]
+    length = extent.astype(jnp.int32)
+    start = KMAX // 2 - length // 2
+    inverse = 1.0 / extent
+    turn = 0.5 * rate * extent
+    for at in range(0, rows, 32):
+        tap = lax.broadcasted_iota(jnp.int32, (32, BLOCK), 0) + (first_tap + at)
+        shifted = tap - start
+        inside = (shifted >= 0) & (shifted < length)
+        centred = (shifted.astype(jnp.float32) - 0.5 * (extent - 1.0)) * inverse
+        square = centred * centred
+        envelope = jnp.where(inside, scale * (0.5 + 0.5 * even_series(square, COS_TERMS)), 0.0)
+        turns = turn * square
+        turns = turns - jnp.floor(turns + 0.5)
+        turn_square = turns * turns
+        real = envelope * even_series(turn_square, COS_TERMS)
+        imag = envelope * (turns * even_series(turn_square, SIN_TERMS))
+        tap_ref[at : at + 32] = real.astype(jnp.bfloat16)
+        tap_ref[rows + at : rows + at + 32] = imag.astype(jnp.bfloat16)
+
+
+def azimuth_kernel(
+    packed_ref,
+    table_ref,
+    forward_ref,
+    spectrum_ref,
+    inverse_ref,
+    out_ref,
+    other,
+    beam,
+    columns,
+    tap_ref,
+    pair_sems,
+    send_sems,
+    recv_sems,
+):
+    tiles = beam.shape[0]
+    tile_here = lax.axis_index("tile")
+    chan_here = lax.axis_index("chan")
+    barrier = pltpu.get_barrier_semaphore()
+    pl.semaphore_signal(barrier, inc=1, device_id={"chan": 1 - chan_here}, device_id_type=MESH)
+    for hop in range(1, tiles):
+        target = lax.rem(tile_here + hop, tiles)
+        pl.semaphore_signal(barrier, inc=1, device_id={"tile": target}, device_id_type=MESH)
+    pl.semaphore_wait(barrier, tiles)
+    swap = pltpu.make_async_remote_copy(
+        src_ref=packed_ref.at[1 - chan_here],
+        dst_ref=other,
+        send_sem=pair_sems.at[0],
+        recv_sem=pair_sems.at[1],
+        device_id={"chan": 1 - chan_here},
+        device_id_type=MESH,
+    )
+    swap.start()
+    pulses = out_ref.shape[1] // 2
+    write_taps(table_ref, tap_ref, KMAX // 2 - pulses)
+    swap.wait()
+    beam[...] = (
+        packed_ref[chan_here].astype(jnp.float32) + other[...].astype(jnp.float32)
+    ).astype(jnp.bfloat16)
+    copies = []
+    for hop in range(1, tiles):
+        target = lax.rem(tile_here + hop, tiles)
+        copy = pltpu.make_async_remote_copy(
+            src_ref=beam.at[target],
+            dst_ref=columns.at[tile_here],
+            send_sem=send_sems.at[hop],
+            recv_sem=recv_sems.at[hop],
+            device_id={"tile": target},
+            device_id_type=MESH,
+        )
+        copy.start()
+        copies.append(copy)
+    columns[tile_here] = beam[tile_here]
+    taps = tap_ref[...]
+    response = jnp.dot(spectrum_ref[0], taps, preferred_element_type=jnp.float32) + jnp.dot(
+        spectrum_ref[1], taps, preferred_element_type=jnp.float32
+    )
+    for copy in copies:
+        copy.wait()
+    signal = columns[...].reshape(2 * pulses, BLOCK)
+    spectrum = jnp.dot(forward_ref[0], signal, preferred_element_type=jnp.float32) + jnp.dot(
+        forward_ref[1], signal, preferred_element_type=jnp.float32
+    )
+    points = 2 * pulses
+    real, imag = spectrum[:points], spectrum[points:]
+    tap_real, tap_imag = response[:points], response[points:]
+    product = jnp.concatenate(
+        [real * tap_real - imag * tap_imag, real * tap_imag + imag * tap_real], 0
+    )
+    high = product.astype(jnp.bfloat16)
+    low = (product - high.astype(jnp.float32)).astype(jnp.bfloat16)
+    over = (((0,), (0,)), ((), ()))
+    result = lax.dot_general(high, inverse_ref[0], over, preferred_element_type=jnp.float32)
+    result += lax.dot_general(low, inverse_ref[0], over, preferred_element_type=jnp.float32)
+    result += lax.dot_general(high, inverse_ref[1], over, preferred_element_type=jnp.float32)
+    out_ref[...] = result[: out_ref.shape[0]]
+
+
+def azimuth_call(packed, table, half_cap):
+    _, tiles, _, local, _ = packed.shape
+    pulses = tiles * local
+    forward, spectrum, inverse = fourier_tables(tiles, pulses)
+    vmem = pl.BlockSpec(memory_space=pltpu.VMEM)
+    return pl.pallas_call(
+        azimuth_kernel,
+        out_shape=jax.ShapeDtypeStruct((half_cap, 2 * pulses), jnp.float32),
+        in_specs=[vmem] * 5,
+        out_specs=vmem,
+        scratch_shapes=[
+            pltpu.VMEM((tiles, 2, local, BLOCK), jnp.bfloat16),
+            pltpu.VMEM((tiles, 2, local, BLOCK), jnp.bfloat16),
+            pltpu.VMEM((tiles, 2, local, BLOCK), jnp.bfloat16),
+            pltpu.VMEM((4 * pulses, BLOCK), jnp.bfloat16),
+            pltpu.SemaphoreType.DMA((2,)),
+            pltpu.SemaphoreType.DMA((tiles,)),
+            pltpu.SemaphoreType.DMA((tiles,)),
+        ],
+        compiler_params=pltpu.CompilerParams(
+            collective_id=0, has_side_effects=True, vmem_limit_bytes=32 << 20
+        ),
+    )(packed, table, jnp.asarray(forward), jnp.asarray(spectrum), jnp.asarray(inverse))
+
+
+def on_device(
+    raw_echoes, range_taps, beam_weights, channel_order, group_cells, tap_counts, chirp_rates
+):
+    tiles = group_cells.shape[0]
+    local, _, _, cell_count = raw_echoes.shape
+    average = cell_count // tiles
+    half_cap = (average + average // 2) // lax.axis_size("chan")
+    fits = average == BLOCK and lax.axis_size("chan") == 2 and 2 * tiles * local == BLOCK
+    if not fits or range_taps.shape[-1] != 2 * BLOCK:
+        return generic_device(
+            raw_echoes,
+            range_taps,
+            beam_weights,
+            channel_order,
+            group_cells,
+            tap_counts,
+            chirp_rates,
+        )
+    packed, table = range_call(
+        raw_echoes,
+        range_taps,
+        beam_weights,
+        channel_order,
+        group_cells,
+        tap_counts,
+        chirp_rates,
+        half_cap,
+    )
+    image = azimuth_call(packed, table, half_cap)
+    return image.reshape(half_cap, 2, tiles * local)
+
+
 def solution(mesh):
     return jax.shard_map(
         on_device,

time: 772 us -> 21 us (0.03); the launches traced: 758 us -> 20.8 us
  local copies, waits for them, and re-layouts: 619 us -> 4.58 us
  other arithmetic: 76.4 us -> 0.11 us
  matrix products: 41.6 us -> 0 us
  Pallas kernels: 0 us -> 15.9 us
  between operations: 14.4 us -> 0.15 us
    another operation x7 -> x0, local copies, waits for them, and re-layouts: 379 us -> none  [the longest x4 206 us: toeplitz_rows(): repeated = jnp.tile(extended, (1,) * len(leading) + (block_len,))]
    reshape x5 -> x1, local copies, waits for them, and re-layouts: 172 us -> 0.78 us  [on_device(): return image.reshape(half_cap, 2, tiles * local)]
    slice x8 -> x3, local copies, waits for them, and re-layouts: 43.8 us -> 1.42 us  [the longest x1 0.83 us: range_call(): range_taps[..., 1:]]
    dot_general x4 -> x0, matrix products: 41.6 us -> none  [the longest x1 36 us: azimuth_focus(): jnp.einsum('sanw,saeiw->seni', windows, matrices, preferred_element_type=...]
    another operation x4 -> x0, other arithmetic: 34.9 us -> none  [the longest x2 34.7 us: complex_matrix(): return jnp.stack([from_real, from_imag], -4)]
    neg x2 -> x0, other arithmetic: 32.4 us -> none  [complex_matrix(): from_imag = jnp.stack([-imag_part, real_part], -3)]
    pallas_call x0 -> x2, Pallas kernels: none -> 15.9 us  [the longest x1 11.9 us: azimuth_call(): pl.pallas_call(azimuth_kernel, out_shape=jax.ShapeDtypeStruct((half_cap,...]
  transfers between devices with their start and end apart: 2 -> 0, of which waited for: 0 -> 0; matrix products, arithmetic and copies ran while one was open for 82% -> 0% of each run, Pallas kernels for 0% -> 0%
where the time goes in v1:
time: 21 us; the launch traced here: 20.8 us
  Pallas kernels  15.9 us (76%)
  local copies, waits for them, and re-layouts  4.58 us (22%)
    pallas_call x1, Pallas kernels, azimuth_call(): pl.pallas_call(azimuth_kernel, out_shape=jax.ShapeDtypeStruct((half_cap,...  11.9 us
    pallas_call x1, Pallas kernels, range_call(): pl.pallas_call(functools.partial(range_kernel, half_cap), grid_spec=pltpu...  4.01 us
    unnamed x19, local copies, waits for them, and re-layouts  2.31 us
    slice x1, local copies, waits for them, and re-layouts, range_call(): range_taps[..., 1:]  0.83 us
    reshape x1, local copies, waits for them, and re-layouts, on_device(): return image.reshape(half_cap, 2, tiles * local)  0.78 us
    slice x2, local copies, waits for them, and re-layouts, range_call(): range_taps[..., :1]  0.59 us

profile of v1, /device:TPU:0, one launch (start us, length us, event | category | flops | bytes accessed | tf_op | source)
XLA Modules:
  0.0 20.8 jit_solution(18151578939081522963)
XLA Ops:
  0.0 0.1 pad.1.clone
  0.1 0.8 %slice.7 = bf16[12,2,511]{2,1,0:T(2,128)(2,1)S(1)} slice(bf16[12,2,512]{2,1,0:T(2,128)(2,1)} %param.11), slice={[0:12], [0:2], [1:512]} | slice | bytes 49056 | tf_op jit(solution)/shard_map/slice | solution.py:284
  0.9 0.5 %reverse = bf16[12,2,512]{2,1,0:T(2,128)(2,1)S(1)} reverse(bf16[12,2,512]{2,1,0:T(2,128)(2,1)S(1)} %bitcast.9), dimensions={2} | reverse | bytes 49152
  1.4 0.0 slice-start
  1.4 0.1 slice.8
  1.5 0.6 %slice-done = bf16[12,2,1]{2,1,0:T(2,128)(2,1)S(1)} async-done(((bf16[12,2,512]{2,1,0:T(2,128)(2,1)}), bf16[12,2,1]{2,1,0:T(2,128)(2,1)S(1)}, s32[]{:S(2)}) %slice-start) | async-done | bytes 72 | tf_op jit(solution)/shard_map/slice | solution.py:282
  2.1 0.0 copy-start.3
  2.1 0.0 copy-start.4
  2.1 0.0 copy-start.5
  2.1 0.0 copy-start.6
  2.1 0.0 copy-start.7
  2.1 0.1 maximum_convert_fusion.filter_ref
  2.2 0.0 copy-start
  2.3 0.0 copy-start.2
  2.3 1.7 %copy.13 = bf16[16,6,2,2048]{3,0,2,1:T(8,128)(2,1)S(1)} copy(bf16[16,6,2,2048]{3,2,1,0:T(2,128)(2,1)} %param.10) | data formatting | bytes 1572864 | tf_op args[0]
  4.0 0.0 copy-start.1
  4.0 0.0 copy-done.3
  4.0 0.0 copy-done.4
  4.0 0.0 copy-done.5
  4.0 0.0 copy-done.6
  4.0 0.0 copy-done.7
  4.0 4.0 %shard_map.100 = (bf16[2,8,2,16,256]{4,3,2,1,0:T(8,128)(2,1)S(1)}, f32[3,8,256]{2,1,0:T(8,128)S(1)}) custom-call(s32[12]{0:T(128)S(1)} %copy-done.6, s32[8]{0:T(128)S(1)} %copy-done.7, bf16[6,2,16,2048]{3,2,1,0:T(8,128)(2,1)S(1)} %bitcast.6, f32[12,2,768]{2,1,0:T(2,128)S(1)} %maximum_convert_fusion.filter_ref, bf16[12,2,2048]{2,1,0:T(2,128)(2,1)S(1)} %copy-done.3, ...), custom_call_target="tpu_custom_call" | custom-call | tf_op jit(solution)/shard_map/pallas_call | solution.py:292
  8.0 0.0 copy-done
  8.0 0.0 copy-done.2
  8.1 0.0 copy-done.1
  8.1 11.9 %shard_map.101 = f32[192,256]{1,0:T(8,128)S(1)} custom-call(bf16[2,8,2,16,256]{4,3,2,1,0:T(8,128)(2,1)S(1)} %get-tuple-element.7.packed_ref, f32[3,8,256]{2,1,0:T(8,128)S(1)} %get-tuple-element.8.table_ref, bf16[2,512,256]{2,1,0:T(8,128)(2,1)S(1)} %copy-done.2, bf16[2,512,512]{2,1,0:T(8,128)(2,1)S(1)} %copy-done, bf16[2,512,256]{2,1,0:T(8,128)(2,1)S(1)} %copy-done.1), custom_call_target="tpu_custom_call" | custom-call | tf_op jit(solution)/shard_map/pallas_call | solution.py:440
  20.0 0.8 %reshape.3 = f32[192,2,128]{2,1,0:T(2,128)} reshape(f32[192,256]{1,0:T(8,128)S(1)} %shard_map.101) | data formatting | bytes 393216 | tf_op jit(solution)/shard_map/reshape | solution.py:489
  (1 shorter events, 0.0 us)
Async XLA Ops:
  1.4 0.7 %slice-start = ((bf16[12,2,512]{2,1,0:T(2,128)(2,1)}), bf16[12,2,1]{2,1,0:T(2,128)(2,1)S(1)}, s32[]{:S(2)}) async-start(bf16[12,2,512]{2,1,0:T(2,128)(2,1)} %param.11), calls=%async_computation | async-start | bytes 12288 | tf_op jit(solution)/shard_map/slice | solution.py:282
  2.1 1.9 %copy-start.3 = (bf16[12,2,2048]{2,1,0:T(2,128)(2,1)S(1)}, bf16[12,2,2048]{2,1,0:T(2,128)(2,1)}, u32[]{:S(2)}) copy-start(bf16[12,2,2048]{2,1,0:T(2,128)(2,1)} %weight_ref.1) | copy-start | bytes 294916
  2.1 1.9 %copy-start.4 = (s32[2048]{0:T(1024)S(1)}, s32[2048]{0:T(1024)}, u32[]{:S(2)}) copy-start(s32[2048]{0:T(1024)} %param.15) | copy-start | bytes 24580
  2.1 1.9 %copy-start.5 = (f32[2048]{0:T(1024)S(1)}, f32[2048]{0:T(1024)}, u32[]{:S(2)}) copy-start(f32[2048]{0:T(1024)} %param.16) | copy-start | bytes 24580
  2.1 1.9 %copy-start.6 = (s32[12]{0:T(128)S(1)}, s32[12]{0:T(128)}, u32[]{:S(2)}) copy-start(s32[12]{0:T(128)} %order_ref.1) | copy-start | bytes 148
  2.1 1.9 %copy-start.7 = (s32[8]{0:T(128)S(1)}, s32[8]{0:T(128)}, u32[]{:S(2)}) copy-start(s32[8]{0:T(128)} %cells_ref.1) | copy-start | bytes 100
  2.2 5.8 %copy-start = (bf16[2,512,512]{2,1,0:T(8,128)(2,1)S(1)}, bf16[2,512,512]{2,1,0:T(8,128)(2,1)}, u32[]{:S(2)}) copy-start(bf16[2,512,512]{2,1,0:T(8,128)(2,1)} %constant.9.clone.spectrum_ref) | copy-start | bytes 3145732
  2.3 5.8 %copy-start.2 = (bf16[2,512,256]{2,1,0:T(8,128)(2,1)S(1)}, bf16[2,512,256]{2,1,0:T(8,128)(2,1)}, u32[]{:S(2)}) copy-start(bf16[2,512,256]{2,1,0:T(8,128)(2,1)} %constant.8.clone.forward_ref) | copy-start | bytes 1572868
  4.0 4.1 %copy-start.1 = (bf16[2,512,256]{2,1,0:T(8,128)(2,1)S(1)}, bf16[2,512,256]{2,1,0:T(8,128)(2,1)}, u32[]{:S(2)}) copy-start(bf16[2,512,256]{2,1,0:T(8,128)(2,1)} %constant.10.clone.inverse_ref) | copy-start | bytes 1572868

commit v2 on v0

--- a/solution.py
+++ b/solution.py
@@ -1,6 +1,11 @@
+import functools
+
 import jax
 import jax.numpy as jnp
+import numpy as np
 from jax import lax
+from jax.experimental import pallas as pl
+from jax.experimental.pallas import tpu as pltpu
 from jax.sharding import PartitionSpec as P
 
 KMAX = 640
@@ -85,7 +90,7 @@
     return jax.vmap(one_group)(group_starts, group_sizes)
 
 
-def on_device(
+def generic_device(
     raw_echoes, range_taps, beam_weights, channel_order, group_cells, tap_counts, chirp_rates
 ):
     local_chans = raw_echoes.shape[1]
@@ -136,6 +141,362 @@
     return azimuth_focus(columns, taps_here)
 
 
+MESH = pl.DeviceIdType.MESH
+BLOCK = 256
+SPAN = 3 * BLOCK
+
+
+def split_bf16(matrix):
+    high = matrix.astype(jnp.bfloat16)
+    low = (matrix - high.astype(np.float64)).astype(jnp.bfloat16)
+    return np.stack([high, low])
+
+
+def fourier_tables(pulses):
+    points = 2 * pulses
+    freq = np.arange(points)[:, None]
+    unit = 2.0 * np.pi / points
+
+    def rotation(index, sign):
+        angle = unit * ((freq * index[None, :]) % points)
+        return np.cos(angle), sign * np.sin(angle)
+
+    cos_x, sin_x = rotation(np.arange(pulses), -1.0)
+    forward = np.block([[cos_x, -sin_x], [sin_x, cos_x]])
+    order = np.arange(2 * pulses).reshape(2, pulses).T.reshape(-1)
+    forward = forward[:, order]
+    cos_h, sin_h = rotation(pulses - np.arange(points), -1.0)
+    taps = np.block([[cos_h, -sin_h], [sin_h, cos_h]])
+    cos_y, sin_y = rotation(np.arange(pulses), 1.0)
+    inverse = np.block([[cos_y, sin_y], [-sin_y, cos_y]]) / points
+    return split_bf16(forward), split_bf16(taps), split_bf16(inverse)
+
+
+def even_series(square, terms):
+    value = jnp.full_like(square, terms[-1])
+    for term in reversed(terms[:-1]):
+        value = value * square + term
+    return value
+
+
+COS_TERMS = [(-1.0) ** n * (2 * np.pi) ** (2 * n) / float(np.prod(np.arange(1, 2 * n + 1, dtype=np.float64))) for n in range(9)]
+SIN_TERMS = [(-1.0) ** n * (2 * np.pi) ** (2 * n + 1) / float(np.prod(np.arange(1, 2 * n + 2, dtype=np.float64))) for n in range(9)]
+
+
+def write_taps(extent, rate, scale, tap_ref, first_tap):
+    rows = tap_ref.shape[0] // 2
+    length = extent.astype(jnp.int32)
+    start = KMAX // 2 - length // 2
+    inverse = 1.0 / extent
+    turn = 0.5 * rate * extent
+    for at in range(0, rows, 32):
+        tap = lax.broadcasted_iota(jnp.int32, (32, BLOCK), 0) + (first_tap + at)
+        shifted = tap - start
+        inside = (shifted >= 0) & (shifted < length)
+        centred = (shifted.astype(jnp.float32) - 0.5 * (extent - 1.0)) * inverse
+        square = centred * centred
+        envelope = jnp.where(inside, scale * (0.5 + 0.5 * even_series(square, COS_TERMS)), 0.0)
+        turns = turn * square
+        turns = turns - jnp.floor(turns + 0.5)
+        turn_square = turns * turns
+        real = envelope * even_series(turn_square, COS_TERMS)
+        imag = envelope * (turns * even_series(turn_square, SIN_TERMS))
+        tap_ref[at : at + 32] = real.astype(jnp.bfloat16)
+        tap_ref[rows + at : rows + at + 32] = imag.astype(jnp.bfloat16)
+
+
+def focus_kernel(
+    half_cap,
+    order_ref,
+    cells_ref,
+    raw_ref,
+    filter_ref,
+    weight_ref,
+    count_ref,
+    rate_ref,
+    forward_ref,
+    spectrum_ref,
+    inverse_ref,
+    out_ref,
+    raw,
+    filters,
+    weights,
+    counts,
+    rates,
+    forward,
+    spectrum,
+    inverse,
+    blocks,
+    mirror,
+    straight,
+    crossed,
+    packed,
+    other,
+    beam,
+    columns,
+    tap_ref,
+    load_sems,
+    raw_sems,
+    pair_sems,
+    send_sems,
+    recv_sems,
+):
+    tiles = beam.shape[0]
+    tile_here = lax.axis_index("tile")
+    chan_here = lax.axis_index("chan")
+    local_chans = raw.shape[0]
+    out_blocks = blocks.shape[0] - 2
+    rows = blocks.shape[1]
+    slots, _, pulses = out_ref.shape
+    points = 2 * pulses
+    barrier = pltpu.get_barrier_semaphore()
+    pl.semaphore_signal(barrier, inc=1, device_id={"chan": 1 - chan_here}, device_id_type=MESH)
+    for hop in range(1, tiles):
+        target = lax.rem(tile_here + hop, tiles)
+        pl.semaphore_signal(barrier, inc=1, device_id={"tile": target}, device_id_type=MESH)
+
+    def fetch(source, target, at):
+        return pltpu.make_async_copy(source, target, load_sems.at[at])
+
+    def fetch_raw(chan):
+        return pltpu.make_async_copy(raw_ref.at[:, chan], raw.at[chan], raw_sems.at[chan])
+
+    get_filters = fetch(filter_ref, filters, 0)
+    get_weights = fetch(weight_ref, weights, 1)
+    late = [
+        fetch(count_ref, counts, 2),
+        fetch(rate_ref, rates, 3),
+        fetch(spectrum_ref, spectrum, 4),
+        fetch(forward_ref, forward, 5),
+        fetch(inverse_ref, inverse, 6),
+    ]
+    get_filters.start()
+    get_weights.start()
+    for chan in range(local_chans):
+        fetch_raw(chan).start()
+    for copy in late:
+        copy.start()
+
+    edge = jnp.zeros((rows, BLOCK), jnp.bfloat16)
+    blocks[0] = edge
+    blocks[out_blocks + 1] = edge
+    straight[...] = jnp.zeros_like(straight)
+    crossed[...] = jnp.zeros_like(crossed)
+    row = lax.broadcasted_iota(jnp.int32, (BLOCK, BLOCK), 0)
+    lane = lax.broadcasted_iota(jnp.int32, (BLOCK, BLOCK), 1)
+    mirror[...] = jnp.where(row + lane == BLOCK - 1, 1.0, 0.0).astype(jnp.bfloat16)
+    get_filters.wait()
+    get_weights.wait()
+
+    def one_channel(chan, carry):
+        physical = order_ref[chan_here * local_chans + chan]
+        own_filter = filters[physical]
+        own_weight = weights[physical].astype(jnp.float32)
+        fetch_raw(chan).wait()
+        for block in range(out_blocks):
+            cells = slice(block * BLOCK, (block + 1) * BLOCK)
+            blocks[block + 1] = raw[chan, :, :, cells].reshape(rows, BLOCK)
+
+        first_half = jnp.dot(
+            own_filter[:, :BLOCK], mirror[...], preferred_element_type=jnp.float32
+        )
+        second_half = jnp.dot(
+            own_filter[:, BLOCK:], mirror[...], preferred_element_type=jnp.float32
+        )
+        backward = jnp.concatenate([jnp.zeros_like(first_half), second_half, first_half], 1)
+
+        def toeplitz(part):
+            row = jnp.broadcast_to(backward[part : part + 1], (128, SPAN))
+            top = pltpu.roll(row, 1, 1, stride=1, stride_axis=0).astype(jnp.bfloat16)
+            low = jnp.concatenate([top[:, SPAN - 128 :], top[:, : SPAN - 128]], 1)
+            return jnp.concatenate([top, low], 0)
+
+        real_rows = toeplitz(0)
+        imag_rows = toeplitz(1)
+        total = None
+        for step in range(3):
+            at = (SPAN - BLOCK * step) % SPAN
+            matrix = jnp.concatenate(
+                [real_rows[:, at : at + BLOCK], imag_rows[:, at : at + BLOCK]], 1
+            )
+            window = blocks[step : step + out_blocks].reshape(out_blocks * rows, BLOCK)
+            term = jnp.dot(window, matrix, preferred_element_type=jnp.float32)
+            total = term if total is None else total + term
+        for block in range(out_blocks):
+            cells = slice(block * BLOCK, (block + 1) * BLOCK)
+            weight_real = own_weight[0:1, cells]
+            weight_imag = own_weight[1:2, cells]
+            by_real = total[block * rows : (block + 1) * rows, :BLOCK]
+            by_imag = total[block * rows : (block + 1) * rows, BLOCK:]
+            straight[block] += weight_real * by_real - weight_imag * by_imag
+            crossed[block] += weight_imag * by_real + weight_real * by_imag
+        return carry
+
+    lax.fori_loop(0, local_chans, one_channel, 0)
+
+    width = 2 * BLOCK
+    is_real = lax.broadcasted_iota(jnp.int32, (rows, BLOCK), 0) % 2 == 0
+
+    def summed(block):
+        turned = crossed[block]
+        return straight[block] + jnp.where(
+            is_real, -pltpu.roll(turned, rows - 1, 0), pltpu.roll(turned, 1, 0)
+        )
+
+    for pair in range(out_blocks // 2):
+        first = cells_ref[2 * pair]
+        values = jnp.concatenate([summed(2 * pair), summed(2 * pair + 1)], 1)
+        moved = pltpu.roll(values, width - first, 1)
+        packed[0, 2 * pair] = values[:, :BLOCK].astype(jnp.bfloat16)
+        packed[0, 2 * pair + 1] = moved[:, :BLOCK].astype(jnp.bfloat16)
+        values = pltpu.roll(values, width - half_cap, 1)
+        moved = pltpu.roll(moved, width - half_cap, 1)
+        packed[1, 2 * pair] = values[:, :BLOCK].astype(jnp.bfloat16)
+        packed[1, 2 * pair + 1] = moved[:, :BLOCK].astype(jnp.bfloat16)
+
+    pl.semaphore_wait(barrier, tiles)
+    swap = pltpu.make_async_remote_copy(
+        src_ref=packed.at[1 - chan_here],
+        dst_ref=other,
+        send_sem=pair_sems.at[0],
+        recv_sem=pair_sems.at[1],
+        device_id={"chan": 1 - chan_here},
+        device_id_type=MESH,
+    )
+    swap.start()
+    for copy in late:
+        copy.wait()
+    offset = chan_here * half_cap
+    begin = offset
+    for tile in range(tiles):
+        begin += jnp.where(tile < tile_here, cells_ref[tile], 0)
+    cell_count = counts.shape[1]
+    shift = lax.rem(2 * cell_count - begin, cell_count)
+
+    def own(table):
+        spread = jnp.broadcast_to(table.astype(jnp.float32), (8, cell_count))
+        return pltpu.roll(spread, shift, 1)[0:1, :BLOCK]
+
+    extent = own(counts[...])
+    slot = lax.broadcasted_iota(jnp.int32, (1, BLOCK), 1)
+    live = (slot < half_cap) & (slot + offset < cells_ref[tile_here])
+    scale = jnp.where(live, 1.6 / jnp.sqrt(extent), 0.0)
+    rate = own(rates[...])
+    swap.wait()
+    beam[...] = (
+        packed[chan_here].astype(jnp.float32) + other[...].astype(jnp.float32)
+    ).astype(jnp.bfloat16)
+    copies = []
+    for hop in range(1, tiles):
+        target = lax.rem(tile_here + hop, tiles)
+        copy = pltpu.make_async_remote_copy(
+            src_ref=beam.at[target],
+            dst_ref=columns.at[tile_here],
+            send_sem=send_sems.at[hop],
+            recv_sem=recv_sems.at[hop],
+            device_id={"tile": target},
+            device_id_type=MESH,
+        )
+        copy.start()
+        copies.append(copy)
+    columns[tile_here] = beam[tile_here]
+    write_taps(extent, rate, scale, tap_ref, KMAX // 2 - pulses)
+    taps = tap_ref[...]
+    response = jnp.dot(spectrum[0], taps, preferred_element_type=jnp.float32) + jnp.dot(
+        spectrum[1], taps, preferred_element_type=jnp.float32
+    )
+    for copy in copies:
+        copy.wait()
+    signal = columns[...].reshape(points, BLOCK)
+    image = jnp.dot(forward[0], signal, preferred_element_type=jnp.float32) + jnp.dot(
+        forward[1], signal, preferred_element_type=jnp.float32
+    )
+    real, imag = image[:points], image[points:]
+    tap_real, tap_imag = response[:points], response[points:]
+    product = jnp.concatenate(
+        [real * tap_real - imag * tap_imag, real * tap_imag + imag * tap_real], 0
+    )
+    high = product.astype(jnp.bfloat16)
+    low = (product - high.astype(jnp.float32)).astype(jnp.bfloat16)
+    over = (((0,), (0,)), ((), ()))
+    result = lax.dot_general(high, inverse[0], over, preferred_element_type=jnp.float32)
+    result += lax.dot_general(low, inverse[0], over, preferred_element_type=jnp.float32)
+    result += lax.dot_general(high, inverse[1], over, preferred_element_type=jnp.float32)
+    out_ref[:, 0, :] = result[:slots, :pulses]
+    out_ref[:, 1, :] = result[:slots, pulses:]
+
+
+def focus_call(raw_echoes, range_taps, beam_weights, order, cells, counts, rates, half_cap):
+    local, local_chans, _, cell_count = raw_echoes.shape
+    tiles = cells.shape[0]
+    pulses = tiles * local
+    rows = 2 * local
+    out_blocks = cell_count // BLOCK
+    tables = [jnp.asarray(table) for table in fourier_tables(pulses)]
+    counts, rates = counts[None], rates[None]
+    arrays = [raw_echoes, range_taps, beam_weights, counts, rates] + tables
+    exchanged = pltpu.VMEM((tiles, rows, BLOCK), jnp.bfloat16)
+    total = pltpu.VMEM((out_blocks, rows, BLOCK), jnp.float32)
+    return pl.pallas_call(
+        functools.partial(focus_kernel, half_cap),
+        out_shape=jax.ShapeDtypeStruct((half_cap, 2, pulses), jnp.float32),
+        in_specs=[pl.BlockSpec(memory_space=pltpu.SMEM)] * 2
+        + [pl.BlockSpec(memory_space=pl.ANY)] * len(arrays),
+        out_specs=pl.BlockSpec(memory_space=pltpu.VMEM),
+        scratch_shapes=[pltpu.VMEM((local_chans, local, 2, cell_count), raw_echoes.dtype)]
+        + [pltpu.VMEM(array.shape, array.dtype) for array in arrays[1:]]
+        + [
+            pltpu.VMEM((out_blocks + 2, rows, BLOCK), jnp.bfloat16),
+            pltpu.VMEM((BLOCK, BLOCK), jnp.bfloat16),
+            total,
+            total,
+            pltpu.VMEM((2, tiles, rows, BLOCK), jnp.bfloat16),
+            exchanged,
+            exchanged,
+            exchanged,
+            pltpu.VMEM((4 * pulses, BLOCK), jnp.bfloat16),
+            pltpu.SemaphoreType.DMA((len(arrays) - 1,)),
+            pltpu.SemaphoreType.DMA((local_chans,)),
+            pltpu.SemaphoreType.DMA((2,)),
+            pltpu.SemaphoreType.DMA((tiles,)),
+            pltpu.SemaphoreType.DMA((tiles,)),
+        ],
+        compiler_params=pltpu.CompilerParams(
+            collective_id=0, has_side_effects=True, vmem_limit_bytes=60 << 20
+        ),
+    )(order, cells, *arrays)
+
+
+def on_device(
+    raw_echoes, range_taps, beam_weights, channel_order, group_cells, tap_counts, chirp_rates
+):
+    tiles = group_cells.shape[0]
+    local, _, _, cell_count = raw_echoes.shape
+    average = cell_count // tiles
+    half_cap = (average + average // 2) // lax.axis_size("chan")
+    fits = average == BLOCK and lax.axis_size("chan") == 2 and 2 * tiles * local == BLOCK
+    if not fits or range_taps.shape[-1] != 2 * BLOCK:
+        return generic_device(
+            raw_echoes,
+            range_taps,
+            beam_weights,
+            channel_order,
+            group_cells,
+            tap_counts,
+            chirp_rates,
+        )
+    return focus_call(
+        raw_echoes,
+        range_taps,
+        beam_weights,
+        channel_order,
+        group_cells,
+        tap_counts,
+        chirp_rates,
+        half_cap,
+    )
+
+
 def solution(mesh):
     return jax.shard_map(
         on_device,

time: 772 us -> 18.7 us (0.02); the launches traced: 758 us -> 18.6 us
  local copies, waits for them, and re-layouts: 619 us -> 1.62 us
  other arithmetic: 76.4 us -> 0 us
  matrix products: 41.6 us -> 0 us
  Pallas kernels: 0 us -> 16.9 us
  between operations: 14.4 us -> 0.01 us
    another operation x7 -> x0, local copies, waits for them, and re-layouts: 379 us -> none  [the longest x4 206 us: toeplitz_rows(): repeated = jnp.tile(extended, (1,) * len(leading) + (block_len,))]
    reshape x5 -> x0, local copies, waits for them, and re-layouts: 172 us -> none  [the longest x2 171 us: toeplitz_rows(): repeated[..., :block_len * span_len]]
    slice x8 -> x0, local copies, waits for them, and re-layouts: 43.8 us -> none  [the longest x2 41.2 us: toeplitz_rows(): repeated[..., :block_len * span_len]]
    dot_general x4 -> x0, matrix products: 41.6 us -> none  [the longest x1 36 us: azimuth_focus(): jnp.einsum('sanw,saeiw->seni', windows, matrices, preferred_element_type=...]
    another operation x4 -> x0, other arithmetic: 34.9 us -> none  [the longest x2 34.7 us: complex_matrix(): return jnp.stack([from_real, from_imag], -4)]
    neg x2 -> x0, other arithmetic: 32.4 us -> none  [complex_matrix(): from_imag = jnp.stack([-imag_part, real_part], -3)]
    pallas_call x0 -> x1, Pallas kernels: none -> 16.9 us  [focus_call(): pl.pallas_call(functools.partial(focus_kernel, half_cap), out_shape=jax.S...]
  transfers between devices with their start and end apart: 2 -> 0, of which waited for: 0 -> 0; matrix products, arithmetic and copies ran while one was open for 82% -> 0% of each run, Pallas kernels for 0% -> 0%
where the time goes in v2:
time: 18.7 us; the launch traced here: 18.6 us
  Pallas kernels  16.9 us (90%)
  local copies, waits for them, and re-layouts  1.62 us (9%)
    pallas_call x1, Pallas kernels, focus_call(): pl.pallas_call(functools.partial(focus_kernel, half_cap), out_shape=jax.S...  16.9 us
    unnamed x1, local copies, waits for them, and re-layouts  1.62 us

profile of v2, /device:TPU:0, one launch (start us, length us, event | category | flops | bytes accessed | tf_op | source)
XLA Modules:
  0.0 18.6 jit_solution(5565594254672295324)
XLA Ops:
  0.0 16.9 %shard_map.100 = f32[192,2,128]{2,1,0:T(2,128)} custom-call(s32[12]{0:T(128)} %order_ref.1, s32[8]{0:T(128)} %cells_ref.1, bf16[16,6,2,2048]{3,2,1,0:T(2,128)(2,1)} %raw_ref.1, bf16[12,2,512]{2,1,0:T(2,128)(2,1)} %filter_ref.1, bf16[12,2,2048]{2,1,0:T(2,128)(2,1)} %weight_ref.1, s32[1,2048]{1,0:T(1,128)} %bitcast.2, f32[1,2048]{1,0:T(1,128)} %bitcast.3, ...), custom_call_target="tpu_custom_call" | custom-call | tf_op jit(solution)/shard_map/pallas_call | solution.py:440
  16.9 1.6 %copy.12 = f32[192,2,128]{2,1,0:T(2,128)} copy(f32[192,2,128]{2,1,0:T(2,128)} %shard_map.100) | data formatting | bytes 393216

commit v3 on v2

--- a/solution.py
+++ b/solution.py
@@ -343,16 +343,29 @@
             is_real, -pltpu.roll(turned, rows - 1, 0), pltpu.roll(turned, 1, 0)
         )
 
+    is_left = lax.broadcasted_iota(jnp.int32, (rows // 2, 128), 1) < 64
+
+    def pack(chan, tile, values):
+        last = values[:, 128:BLOCK]
+        folded = jnp.where(is_left, last[: rows // 2], pltpu.roll(last[rows // 2 :], 64, 1))
+        packed[chan, tile, :rows] = values[:, :128].astype(jnp.bfloat16)
+        packed[chan, tile, rows:] = folded.astype(jnp.bfloat16)
+
+    def unpack(block):
+        folded = block[rows:]
+        turned = pltpu.roll(folded.astype(jnp.float32), 64, 1).astype(jnp.bfloat16)
+        return jnp.concatenate([block[:rows], jnp.concatenate([folded, turned], 0)], 1)
+
     for pair in range(out_blocks // 2):
         first = cells_ref[2 * pair]
         values = jnp.concatenate([summed(2 * pair), summed(2 * pair + 1)], 1)
         moved = pltpu.roll(values, width - first, 1)
-        packed[0, 2 * pair] = values[:, :BLOCK].astype(jnp.bfloat16)
-        packed[0, 2 * pair + 1] = moved[:, :BLOCK].astype(jnp.bfloat16)
+        pack(0, 2 * pair, values)
+        pack(0, 2 * pair + 1, moved)
         values = pltpu.roll(values, width - half_cap, 1)
         moved = pltpu.roll(moved, width - half_cap, 1)
-        packed[1, 2 * pair] = values[:, :BLOCK].astype(jnp.bfloat16)
-        packed[1, 2 * pair + 1] = moved[:, :BLOCK].astype(jnp.bfloat16)
+        pack(1, 2 * pair, values)
+        pack(1, 2 * pair + 1, moved)
 
     pl.semaphore_wait(barrier, tiles)
     swap = pltpu.make_async_remote_copy(
@@ -407,7 +420,7 @@
     )
     for copy in copies:
         copy.wait()
-    signal = columns[...].reshape(points, BLOCK)
+    signal = jnp.concatenate([unpack(columns[tile]) for tile in range(tiles)], 0)
     image = jnp.dot(forward[0], signal, preferred_element_type=jnp.float32) + jnp.dot(
         forward[1], signal, preferred_element_type=jnp.float32
     )
@@ -435,11 +448,11 @@
     tables = [jnp.asarray(table) for table in fourier_tables(pulses)]
     counts, rates = counts[None], rates[None]
     arrays = [raw_echoes, range_taps, beam_weights, counts, rates] + tables
-    exchanged = pltpu.VMEM((tiles, rows, BLOCK), jnp.bfloat16)
+    exchanged = pltpu.VMEM((tiles, 3 * rows // 2, 128), jnp.bfloat16)
     total = pltpu.VMEM((out_blocks, rows, BLOCK), jnp.float32)
     return pl.pallas_call(
         functools.partial(focus_kernel, half_cap),
-        out_shape=jax.ShapeDtypeStruct((half_cap, 2, pulses), jnp.float32),
+        out_shape=pltpu.VMEM((half_cap, 2, pulses), jnp.float32),
         in_specs=[pl.BlockSpec(memory_space=pltpu.SMEM)] * 2
         + [pl.BlockSpec(memory_space=pl.ANY)] * len(arrays),
         out_specs=pl.BlockSpec(memory_space=pltpu.VMEM),
@@ -450,7 +463,7 @@
             pltpu.VMEM((BLOCK, BLOCK), jnp.bfloat16),
             total,
             total,
-            pltpu.VMEM((2, tiles, rows, BLOCK), jnp.bfloat16),
+            pltpu.VMEM((2, tiles, 3 * rows // 2, 128), jnp.bfloat16),
             exchanged,
             exchanged,
             exchanged,
@@ -462,7 +475,7 @@
             pltpu.SemaphoreType.DMA((tiles,)),
         ],
         compiler_params=pltpu.CompilerParams(
-            collective_id=0, has_side_effects=True, vmem_limit_bytes=60 << 20
+            collective_id=0, has_side_effects=True, vmem_limit_bytes=56 << 20
         ),
     )(order, cells, *arrays)
 

time: 18.7 us -> 17 us (0.909)
  local copies, waits for them, and re-layouts: 1.62 us -> 0.68 us
  Pallas kernels: 16.9 us -> 16.2 us
    unnamed x1, local copies, waits for them, and re-layouts: 1.62 us -> 0.68 us
    pallas_call x1, Pallas kernels: 16.9 us -> 16.2 us  [focus_call(): pl.pallas_call(functools.partial(focus_kernel, half_cap), out_shape=pltpu...]
where the time goes in v3:
time: 17 us; the launch traced here: 16.9 us
  Pallas kernels  16.2 us (95%)
  local copies, waits for them, and re-layouts  0.68 us (4%)
    pallas_call x1, Pallas kernels, focus_call(): pl.pallas_call(functools.partial(focus_kernel, half_cap), out_shape=pltpu...  16.2 us
    unnamed x1, local copies, waits for them, and re-layouts  0.68 us

profile of v3, /device:TPU:0, one launch (start us, length us, event | category | flops | bytes accessed | tf_op | source)
XLA Modules:
  0.0 16.9 jit_solution(4360793785418555718)
XLA Ops:
  0.0 16.2 %shard_map.100 = f32[192,2,128]{2,1,0:T(2,128)S(1)} custom-call(s32[12]{0:T(128)} %order_ref.1, s32[8]{0:T(128)} %cells_ref.1, bf16[16,6,2,2048]{3,2,1,0:T(2,128)(2,1)} %raw_ref.1, bf16[12,2,512]{2,1,0:T(2,128)(2,1)} %filter_ref.1, bf16[12,2,2048]{2,1,0:T(2,128)(2,1)} %weight_ref.1, s32[1,2048]{1,0:T(1,128)} %bitcast.2, f32[1,2048]{1,0:T(1,128)} %bitcast.3, ...), custom_call_target="tpu_custom_call" | custom-call | tf_op jit(solution)/shard_map/pallas_call | solution.py:453
  16.2 0.7 %copy.12 = f32[192,2,128]{2,1,0:T(2,128)} copy(f32[192,2,128]{2,1,0:T(2,128)S(1)} %shard_map.100) | data formatting | bytes 393216

commit v4 on v3

--- a/solution.py
+++ b/solution.py
@@ -207,8 +207,8 @@
 
 def focus_kernel(
     half_cap,
-    order_ref,
-    cells_ref,
+    order_hbm,
+    cells_hbm,
     raw_ref,
     filter_ref,
     weight_ref,
@@ -218,6 +218,8 @@
     spectrum_ref,
     inverse_ref,
     out_ref,
+    order_ref,
+    cells_ref,
     raw,
     filters,
     weights,
@@ -270,6 +272,10 @@
         fetch(forward_ref, forward, 5),
         fetch(inverse_ref, inverse, 6),
     ]
+    get_order = fetch(order_hbm, order_ref, 7)
+    get_cells = fetch(cells_hbm, cells_ref, 8)
+    get_order.start()
+    get_cells.start()
     get_filters.start()
     get_weights.start()
     for chan in range(local_chans):
@@ -285,6 +291,8 @@
     row = lax.broadcasted_iota(jnp.int32, (BLOCK, BLOCK), 0)
     lane = lax.broadcasted_iota(jnp.int32, (BLOCK, BLOCK), 1)
     mirror[...] = jnp.where(row + lane == BLOCK - 1, 1.0, 0.0).astype(jnp.bfloat16)
+    get_order.wait()
+    get_cells.wait()
     get_filters.wait()
     get_weights.wait()
 
@@ -453,10 +461,10 @@
     return pl.pallas_call(
         functools.partial(focus_kernel, half_cap),
         out_shape=pltpu.VMEM((half_cap, 2, pulses), jnp.float32),
-        in_specs=[pl.BlockSpec(memory_space=pltpu.SMEM)] * 2
-        + [pl.BlockSpec(memory_space=pl.ANY)] * len(arrays),
+        in_specs=[pl.BlockSpec(memory_space=pl.ANY)] * (2 + len(arrays)),
         out_specs=pl.BlockSpec(memory_space=pltpu.VMEM),
-        scratch_shapes=[pltpu.VMEM((local_chans, local, 2, cell_count), raw_echoes.dtype)]
+        scratch_shapes=[pltpu.SMEM(order.shape, order.dtype), pltpu.SMEM(cells.shape, cells.dtype)]
+        + [pltpu.VMEM((local_chans, local, 2, cell_count), raw_echoes.dtype)]
         + [pltpu.VMEM(array.shape, array.dtype) for array in arrays[1:]]
         + [
             pltpu.VMEM((out_blocks + 2, rows, BLOCK), jnp.bfloat16),
@@ -468,7 +476,7 @@
             exchanged,
             exchanged,
             pltpu.VMEM((4 * pulses, BLOCK), jnp.bfloat16),
-            pltpu.SemaphoreType.DMA((len(arrays) - 1,)),
+            pltpu.SemaphoreType.DMA((len(arrays) + 1,)),
             pltpu.SemaphoreType.DMA((local_chans,)),
             pltpu.SemaphoreType.DMA((2,)),
             pltpu.SemaphoreType.DMA((tiles,)),

time: 17 us -> 16.3 us (0.959)
  Pallas kernels: 16.2 us -> 15.4 us
    pallas_call x1, Pallas kernels: 16.2 us -> 15.4 us  [focus_call(): pl.pallas_call(functools.partial(focus_kernel, half_cap), out_shape=pltpu...]
where the time goes in v4:
time: 16.3 us; the launch traced here: 16.1 us
  Pallas kernels  15.4 us (94%)
  local copies, waits for them, and re-layouts  0.68 us (4%)
    pallas_call x1, Pallas kernels, focus_call(): pl.pallas_call(functools.partial(focus_kernel, half_cap), out_shape=pltpu...  15.4 us
    unnamed x1, local copies, waits for them, and re-layouts  0.68 us

profile of v4, /device:TPU:0, one launch (start us, length us, event | category | flops | bytes accessed | tf_op | source)
XLA Modules:
  0.0 16.1 jit_solution(15680075192684850397)
XLA Ops:
  0.0 15.4 %shard_map.100 = f32[192,2,128]{2,1,0:T(2,128)S(1)} custom-call(s32[12]{0:T(128)} %order_hbm.1, s32[8]{0:T(128)} %cells_hbm.1, bf16[16,6,2,2048]{3,2,1,0:T(2,128)(2,1)} %raw_ref.1, bf16[12,2,512]{2,1,0:T(2,128)(2,1)} %filter_ref.1, bf16[12,2,2048]{2,1,0:T(2,128)(2,1)} %weight_ref.1, s32[1,2048]{1,0:T(1,128)} %bitcast.2, f32[1,2048]{1,0:T(1,128)} %bitcast.3, ...), custom_call_target="tpu_custom_call" | custom-call | tf_op jit(solution)/shard_map/pallas_call | solution.py:461
  15.4 0.7 %copy.12 = f32[192,2,128]{2,1,0:T(2,128)} copy(f32[192,2,128]{2,1,0:T(2,128)S(1)} %shard_map.100) | data formatting | bytes 393216
